TPU v7x, 32 devices: a whole 2x2x4 slice. The times are simulated.
32 devices in a mesh: groups: 2 (over y), snap: 4 (over z), slab: 2 (over x), sub: 2 (over core).
Axes of the slice: x: 2, y: 2, z: 4, core: 2. Of those that a mesh axis runs over, the one named last changes fastest.
Arguments:
- fields: float32 [8, 4, 4, 16, 128], P(('groups', 'snap'), None, 'slab', 'sub'), parts along dimension 0, may hold values from -18 to 18
- snap_ids: int32 [8], P(('groups', 'snap')), parts along dimension 0, may hold values from 0 to 63
- snap_weight: float32 [64], replicated, may hold values from 0.5 to 2
- product_terms: int32 [192, 3], replicated, may hold values from 0 to 27, as said below
- mix_weight: float32 [192], replicated, may hold values from -1.5 to 1.5
Outputs:
- whitened: bfloat16 [8, 192, 4, 16, 128], P(('groups', 'snap'), None, 'slab', 'sub'), parts along dimension 0
- r_factor: float32 [384, 192], P('groups'), parts along dimension 0
There are 2 independent parts, one for each index of `groups`. A program takes and returns all parts, laid end to end along the dimension named above; an argument that names none is the same for every part. Nothing has to cross between parts.
Inputs may be any that keep to these rules, and one draw needn't show every extreme that they name: `product_terms`: each row names three different bases, and no two rows are equal.
All inputs are finite; a program needn't handle non-finite values.
Results may differ from a plain program's by a relative error of at most 0.0028.
Values sent between devices are 32-bit elements; how exact they have to be, the bound alone decides.
A program may use at most 64 MiB of HBM per device.

v0:
```python
import jax
import jax.numpy as jnp
from jax import lax
from jax.sharding import PartitionSpec as P

ridge_value = 0.05


def padded_2(block, sides, width):
    for axis, dim in sides:
        count = lax.axis_size(axis)
        forward = [(i, i + 1) for i in range(count - 1)]
        forward.append((count - 1, 0))
        backward = [(target, source) for source, target in forward]
        low = lax.ppermute(
            lax.slice_in_dim(block, block.shape[dim] - width, None, axis=dim), axis, forward
        )
        high = lax.ppermute(lax.slice_in_dim(block, 0, width, axis=dim), axis, backward)
        block = jnp.concatenate([low, block, high], axis=dim)
    return block


def stencil_pair(values, ahead_one, behind_one, ahead_two, behind_two):
    first_deriv = (8.0 * (ahead_one - behind_one) - (ahead_two - behind_two)) / 12.0
    second_deriv = (
        16.0 * (ahead_one + behind_one) - (ahead_two + behind_two) - 30.0 * values
    ) / 12.0
    return (first_deriv, second_deriv)


def dot_highest(left_matrix, right_matrix):
    return jnp.dot(left_matrix, right_matrix, precision=lax.Precision.HIGHEST)


def upper_cholesky(matrix):
    order = matrix.shape[0]
    positions = jnp.arange(order, dtype=jnp.int32)

    def column_step(step, state):
        work, upper = state
        row_now = lax.dynamic_slice_in_dim(work, step, 1, 0)[0]
        pivot = lax.dynamic_slice_in_dim(row_now, step, 1, 0)[0]
        scaled = jnp.where(positions >= step, row_now / jnp.sqrt(pivot), 0.0)
        work = work - scaled[:, None] * scaled[None, :]
        upper = lax.dynamic_update_slice_in_dim(upper, scaled[None, :], step, 0)
        return (work, upper)

    start = (matrix, jnp.zeros_like(matrix))
    return lax.fori_loop(0, order, column_step, start)[1]


def transposed_solve(upper, right_side):
    order = upper.shape[0]
    positions = jnp.arange(order, dtype=jnp.int32)

    def row_step(step, solved):
        column = lax.dynamic_slice_in_dim(upper, step, 1, 1)[:, 0]
        pivot = lax.dynamic_slice_in_dim(column, step, 1, 0)[0]
        masked = jnp.where(positions < step, column, 0.0)
        target = lax.dynamic_slice_in_dim(right_side, step, 1, 0)
        row_new = (target - dot_highest(masked[None, :], solved)) / pivot
        return lax.dynamic_update_slice_in_dim(solved, row_new, step, 0)

    return lax.fori_loop(0, order, row_step, jnp.zeros_like(right_side))


def local(fields, snap_ids, snap_weight, product_terms, mix_weight):
    padded = padded_2(fields, (("slab", 2), ("sub", 3)), 2)
    layers = fields.shape[2]
    columns = fields.shape[3]
    center = padded[0, :, 2 : 2 + layers, 2 : 2 + columns, :]

    def along_z(offset):
        return padded[0, :, 2 + offset : 2 + offset + layers, 2 : 2 + columns, :]

    def along_x(offset):
        return padded[0, :, 2 : 2 + layers, 2 + offset : 2 + offset + columns, :]

    z_first, z_second = stencil_pair(center, along_z(1), along_z(-1), along_z(2), along_z(-2))
    x_first, x_second = stencil_pair(center, along_x(1), along_x(-1), along_x(2), along_x(-2))
    y_first, y_second = stencil_pair(
        center,
        jnp.roll(center, -1, 3),
        jnp.roll(center, 1, 3),
        jnp.roll(center, -2, 3),
        jnp.roll(center, 2, 3),
    )
    stacked = jnp.stack([center, z_first, x_first, y_first, z_second, x_second, y_second], axis=1)
    base_count = stacked.shape[0] * stacked.shape[1]
    bases = stacked.reshape(base_count, -1)
    table_size = snap_weight.shape[0]
    snap_scale = jnp.sum(jnp.where(jnp.arange(table_size) == snap_ids[0], snap_weight, 0.0))
    feature_count = product_terms.shape[0]
    choose = (product_terms.T.reshape(-1)[:, None] == jnp.arange(base_count)[None, :]).astype(
        jnp.float32
    )
    picked = dot_highest(choose, bases)
    left_term = picked[:feature_count]
    middle = picked[feature_count : 2 * feature_count]
    right_term = picked[2 * feature_count :]
    features = snap_scale * left_term * (middle + mix_weight[:, None] * right_term)
    local_gram = lax.dot_general(
        features, features, (((1,), (1,)), ((), ())), precision=lax.Precision.HIGHEST
    )
    cells_total = float(
        lax.axis_size("snap") * lax.axis_size("slab") * lax.axis_size("sub") * bases.shape[1]
    )
    identity = jnp.eye(feature_count, dtype=jnp.float32)
    total_gram = lax.psum(local_gram, ("snap", "slab", "sub"))
    r_factor = upper_cholesky(total_gram / cells_total + ridge_value * identity)
    inverse = transposed_solve(r_factor, identity)
    solved = dot_highest(inverse, features)
    whitened = solved.reshape(1, feature_count, layers, columns, -1).astype(jnp.bfloat16)
    return (whitened, r_factor)


def solution(mesh):
    return jax.shard_map(
        local,
        mesh=mesh,
        in_specs=(
            P(("groups", "snap"), None, "slab", "sub", None),
            P(("groups", "snap")),
            P(),
            P(),
            P(),
        ),
        out_specs=(P(("groups", "snap"), None, "slab", "sub", None), P("groups", None)),
        check_vma=False,
    )
```

profile of v0, /device:TPU:0, one launch (start us, length us, event | category | flops | bytes accessed | tf_op | source)
XLA Modules:
  0.0 691.6 jit_solution(17361808163700659640)
XLA Ops:
  7.2 3.0 collective-permute-start.1
  10.3 0.8 bitcast_dynamic-update-slice_fusion.2
  11.1 0.9 slice_bitcast_fusion.7
  12.0 0.9 slice_bitcast_fusion.6
  12.9 0.9 slice_bitcast_fusion.3
  13.9 0.9 slice_bitcast_fusion.2
  15.4 1.3 fusion.15
  16.7 0.8 eq.29
  17.5 0.8 constant_dynamic-update-slice_fusion.1
  18.8 0.7 bitcast_dynamic-update-slice_fusion.1
  20.1 2.1 fusion.8
  22.2 1.0 fusion.6
  23.2 2.1 fusion.17
  25.3 92.5 %all-reduce.2.cloned.1.call-done = f32[192,192]{1,0:T(8,128)} async-done(((f32[192,192]{1,0:T(8,128)}), f32[192,192]{1,0:T(8,128)}) %all-reduce.2.cloned.1.call-update) | async-done | bytes 147472 | tf_op jit(solution)/shard_map/psum | solution.py:109
  117.8 0.9 select_add_fusion
  118.8 288.9 %while.36 = (s32[]{:T(128)}, f32[192,192]{1,0:T(8,128)S(1)}, f32[192,192]{1,0:T(8,128)S(1)}, s32[]{:T(128)}, s32[]{:T(128)}, /*index=5*/s32[]{:T(128)}) while((s32[]{:T(128)}, f32[192,192]{1,0:T(8,128)S(1)}, f32[192,192]{1,0:T(8,128)S(1)}, s32[]{:T(128)}, s32[]{:T(128)}, /*index=5*/s32[]{:T(128)}) %tuple.96), condition=%wide.region_3.4_spmd.clone, body=%wide.region_2.3_spmd.clone.sunk | while | flops 74691 | bytes 302333 | solution.py:49
  407.9 274.4 %while.37 = (s32[]{:T(128)}, f32[192,192]{1,0:T(8,128)S(1)}, f32[192,192]{1,0:T(8,128)S(1)}, f32[192,192]{0,1:T(8,128)S(1)}, s32[]{:T(128)}, /*index=5*/s32[]{:T(128)}, s32[]{:T(128)}) while((s32[]{:T(128)}, f32[192,192]{1,0:T(8,128)S(1)}, f32[192,192]{1,0:T(8,128)S(1)}, f32[192,192]{0,1:T(8,128)S(1)}, s32[]{:T(128)}, ...), condition=%wide.region_5.6_spmd.clone, body=%wide.region_4.5_spmd.clone.sunk | while | flops 443139 | bytes 154493 | solution.py:64
  411.4 0.7 fusion.30
  415.7 0.7 fusion.30
  420.0 0.7 fusion.30
  422.8 0.7 fusion.30
  427.1 0.7 fusion.30
  431.4 0.7 fusion.30
  438.5 0.7 fusion.30
  442.8 0.7 fusion.30
  447.1 0.7 fusion.30
  450.0 0.7 fusion.30
  454.3 0.7 fusion.30
  458.5 0.7 fusion.30
  465.7 0.7 fusion.30
  682.2 1.5 fusion.7
  683.7 1.1 copy.23
  (2128 shorter events, 403.6 us)
Async XLA Ops:
  7.2 12.7 %copy-start = (f32[1,4,2,8,128]{4,3,2,1,0:T(8,128)S(1)}, f32[1,4,2,8,128]{4,3,2,1,0:T(8,128)}, u32[]{:S(2)}) copy-start(f32[1,4,2,8,128]{4,3,2,1,0:T(8,128)} %param.9) | copy-start | bytes 98308
  7.2 110.7 %all-reduce.2.cloned.1.call-start = ((), (), s32[]{:S(2)}) async-start(), calls=%async_computation | async-start | bytes 393216 | tf_op jit(solution)/shard_map/psum | solution.py:109
  7.2 10.2 %collective-permute-start.1 = (f32[1,4,2,8,128]{4,3,2,1,0:T(8,128)}, f32[1,4,2,8,128]{4,3,2,1,0:T(8,128)S(1)}, u32[]{:S(2)}, u32[]{:S(2)}) collective-permute-start(f32[1,4,2,8,128]{4,3,2,1,0:T(8,128)} %param.9), channel_id=1, source_target_pairs={{0,2},{2,0},{1,3},{3,1},{4,6},{6,4},{5,7},{7,5},{8,10},{10,8},{9,1... | collective-permute-start | bytes 98312 | tf_op jit(solution)/shard_map/ppermute | solution.py:15
  10.3 8.0 %collective-permute-start = (f32[1,4,2,8,128]{4,3,2,1,0:T(8,128)}, f32[1,4,2,8,128]{4,3,2,1,0:T(8,128)S(1)}, u32[]{:S(2)}, u32[]{:S(2)}) collective-permute-start(f32[1,4,2,8,128]{4,3,2,1,0:T(8,128)} %param.9), channel_id=1, source_target_pairs={{2,0},{0,2},{3,1},{1,3},{6,4},{4,6},{7,5},{5,7},{10,8},{8,10},{11,... | collective-permute-start | bytes 98312 | tf_op jit(solution)/shard_map/ppermute | solution.py:18
  18.3 1.3 collective-permute-start.2
  18.3 1.3 collective-permute-start.3
  20.1 2.1 copy-start.2
  407.7 276.0 %copy-start.1 = (f32[192,192]{1,0:T(8,128)}, f32[192,192]{1,0:T(8,128)S(1)}, u32[]{:S(2)}) copy-start(f32[192,192]{1,0:T(8,128)S(1)} %get-tuple-element.297) | copy-start | bytes 442372
Sparse Core Ops, SparseCore 0:
  25.4 92.3 all-reduce.1
where the time goes:
time: 696 us; the launch traced here: 692 us
  local copies, waits for them, and re-layouts  254 us (36%)
  loops' own time  151 us (22%)
  matrix products  146 us (21%)
  waiting for transfers between devices  92.6 us (13%)
  other arithmetic  29.2 us (4%)
  between operations  14.9 us (2%)
    dot_general x194, matrix products, dot_highest(): return jnp.dot(left_matrix, right_matrix, precision=lax.Precision.HIGHEST)  144 us
    another operation x1, loops' own time, upper_cholesky(): return lax.fori_loop(0, order, column_step, start)[1]  143 us
    dynamic_slice x192, local copies, waits for them, and re-layouts, row_step(): pivot = lax.dynamic_slice_in_dim(column, step, 1, 0)[0]  114 us
    dynamic_slice x192, local copies, waits for them, and re-layouts, column_step(): pivot = lax.dynamic_slice_in_dim(row_now, step, 1, 0)[0]  113 us
    psum x1, waiting for transfers between devices, local(): total_gram = lax.psum(local_gram, ('snap', 'slab', 'sub'))  92.5 us
    sub x192, other arithmetic, column_step(): work = work - scaled[:, None] * scaled[None, :]  19.5 us
  transfers between devices with their start and end apart: 5, of which 2 were waited for; matrix products, arithmetic and copies ran while one was open for 1% of the time, Pallas kernels for 0%

commit v1 on v0

--- a/solution.py
+++ b/solution.py
@@ -1,9 +1,13 @@
 import jax
 import jax.numpy as jnp
 from jax import lax
+from jax.experimental import pallas as pl
+from jax.experimental.pallas import tpu as pltpu
 from jax.sharding import PartitionSpec as P
 
 ridge_value = 0.05
+panel_rows = 32
+HIGHEST = lax.Precision.HIGHEST
 
 
 def padded_2(block, sides, width):
@@ -29,39 +33,58 @@
 
 
 def dot_highest(left_matrix, right_matrix):
-    return jnp.dot(left_matrix, right_matrix, precision=lax.Precision.HIGHEST)
+    return jnp.dot(left_matrix, right_matrix, precision=HIGHEST)
 
 
-def upper_cholesky(matrix):
-    order = matrix.shape[0]
-    positions = jnp.arange(order, dtype=jnp.int32)
-
-    def column_step(step, state):
-        work, upper = state
-        row_now = lax.dynamic_slice_in_dim(work, step, 1, 0)[0]
-        pivot = lax.dynamic_slice_in_dim(row_now, step, 1, 0)[0]
-        scaled = jnp.where(positions >= step, row_now / jnp.sqrt(pivot), 0.0)
-        work = work - scaled[:, None] * scaled[None, :]
-        upper = lax.dynamic_update_slice_in_dim(upper, scaled[None, :], step, 0)
-        return (work, upper)
-
-    start = (matrix, jnp.zeros_like(matrix))
-    return lax.fori_loop(0, order, column_step, start)[1]
+def eliminate(work, order):
+    half = work.shape[1] // 2
+    for start in range(0, order, panel_rows):
+        stop = start + panel_rows
+        low = start // 128 * 128
+        high = half + (stop + 127) // 128 * 128
+        panel = work[start:stop, low:high]
+        row_index = lax.broadcasted_iota(jnp.int32, (panel_rows, 1), 0)
+        pivots = jnp.ones((panel_rows, 1), jnp.float32)
+        for step in range(panel_rows):
+            place = start + step - low
+            row = panel[step : step + 1, :]
+            pivot = panel[step : step + 1, place : place + 1]
+            pivots = jnp.where(row_index == step, pivot, pivots)
+            if step + 1 < panel_rows:
+                column = panel[:, place : place + 1] * (1.0 / pivot)
+                panel = panel - jnp.where(row_index > step, column, 0.0) * row
+        panel = panel * (1.0 / jnp.sqrt(pivots))
+        work[start:stop, low:high] = panel
+        if stop < order:
+            sides = panel[:, : half - low].T[stop - low : order - low, :]
+            work[stop:order, low:high] = work[stop:order, low:high] - jnp.dot(
+                sides, panel, precision=HIGHEST, preferred_element_type=jnp.float32
+            )
 
 
-def transposed_solve(upper, right_side):
-    order = upper.shape[0]
-    positions = jnp.arange(order, dtype=jnp.int32)
-
-    def row_step(step, solved):
-        column = lax.dynamic_slice_in_dim(upper, step, 1, 1)[:, 0]
-        pivot = lax.dynamic_slice_in_dim(column, step, 1, 0)[0]
-        masked = jnp.where(positions < step, column, 0.0)
-        target = lax.dynamic_slice_in_dim(right_side, step, 1, 0)
-        row_new = (target - dot_highest(masked[None, :], solved)) / pivot
-        return lax.dynamic_update_slice_in_dim(solved, row_new, step, 0)
-
-    return lax.fori_loop(0, order, row_step, jnp.zeros_like(right_side))
+def whiten_kernel(cells_total, gram_ref, feature_ref, white_ref, factor_ref, work, spread):
+    order = gram_ref.shape[0]
+    half = work.shape[1] // 2
+    rows = lax.broadcasted_iota(jnp.int32, (order, order), 0)
+    columns = lax.broadcasted_iota(jnp.int32, (order, order), 1)
+    identity = (rows == columns).astype(jnp.float32)
+    work[...] = jnp.zeros_like(work)
+    work[:, :order] = gram_ref[...] * (1.0 / cells_total) + ridge_value * identity
+    work[:, half : half + order] = identity
+    eliminate(work, order)
+    factor_ref[...] = jnp.where(columns >= rows, work[:, :order], 0.0)
+    inverse = jnp.where(columns <= rows, work[:, half : half + order], 0.0)
+    tiles = feature_ref.shape[1] // 128
+    for tile in range(0, tiles, 2):
+        solved = jnp.dot(
+            inverse,
+            feature_ref[:, tile * 128 : tile * 128 + 256],
+            precision=HIGHEST,
+            preferred_element_type=jnp.float32,
+        )
+        spread[pl.ds(tile, order, stride=tiles), :] = solved[:, :128]
+        spread[pl.ds(tile + 1, order, stride=tiles), :] = solved[:, 128:]
+    white_ref[...] = spread[...].reshape(white_ref.shape).astype(white_ref.dtype)
 
 
 def local(fields, snap_ids, snap_weight, product_terms, mix_weight):
@@ -100,17 +123,28 @@
     right_term = picked[2 * feature_count :]
     features = snap_scale * left_term * (middle + mix_weight[:, None] * right_term)
     local_gram = lax.dot_general(
-        features, features, (((1,), (1,)), ((), ())), precision=lax.Precision.HIGHEST
+        features, features, (((1,), (1,)), ((), ())), precision=HIGHEST
     )
+    cells = bases.shape[1]
     cells_total = float(
-        lax.axis_size("snap") * lax.axis_size("slab") * lax.axis_size("sub") * bases.shape[1]
+        lax.axis_size("snap") * lax.axis_size("slab") * lax.axis_size("sub") * cells
     )
-    identity = jnp.eye(feature_count, dtype=jnp.float32)
     total_gram = lax.psum(local_gram, ("snap", "slab", "sub"))
-    r_factor = upper_cholesky(total_gram / cells_total + ridge_value * identity)
-    inverse = transposed_solve(r_factor, identity)
-    solved = dot_highest(inverse, features)
-    whitened = solved.reshape(1, feature_count, layers, columns, -1).astype(jnp.bfloat16)
+    import functools
+
+    whitened, r_factor = pl.pallas_call(
+        functools.partial(whiten_kernel, cells_total),
+        out_shape=(
+            jax.ShapeDtypeStruct((1, feature_count, layers, columns, fields.shape[4]), jnp.bfloat16),
+            jax.ShapeDtypeStruct((feature_count, feature_count), jnp.float32),
+        ),
+        in_specs=[pl.BlockSpec(memory_space=pltpu.VMEM)] * 2,
+        out_specs=(pl.BlockSpec(memory_space=pltpu.VMEM),) * 2,
+        scratch_shapes=[
+            pltpu.VMEM((feature_count, 512), jnp.float32),
+            pltpu.VMEM((feature_count * (cells // 128), 128), jnp.float32),
+        ],
+    )(total_gram, features)
     return (whitened, r_factor)
 
 

time: 696 us -> 148 us (0.21)
  local copies, waits for them, and re-layouts: 254 us -> 6.01 us
  loops' own time: 151 us -> 0 us
  matrix products: 146 us -> 4.18 us
  other arithmetic: 29.2 us -> 3.39 us
  Pallas kernels: 0 us -> 22.2 us
    dynamic_slice x576 -> x0, local copies, waits for them, and re-layouts: 229 us -> none  [the longest x192 114 us: row_step(): pivot = lax.dynamic_slice_in_dim(column, step, 1, 0)[0]]
    another operation x2 -> x0, loops' own time: 151 us -> none  [the longest x1 143 us: upper_cholesky(): return lax.fori_loop(0, order, column_step, start)[1]]
    dot_general x195 -> x2, matrix products: 146 us -> 4.18 us  [the longest x1 2.11 us: local(): lax.dot_general(features, features, (((1,), (1,)), ((), ())), precision=H...]
    pallas_call x0 -> x1, Pallas kernels: none -> 22.2 us  [local(): pl.pallas_call(functools.partial(whiten_kernel, cells_total), out_shape=(...]
    sub x192 -> x0, other arithmetic: 19.5 us -> none  [column_step(): work = work - scaled[:, None] * scaled[None, :]]
    dynamic_update_slice x384 -> x0, local copies, waits for them, and re-layouts: 17.7 us -> none  [the longest x192 9.5 us: row_step(): return lax.dynamic_update_slice_in_dim(solved, row_new, step, 0)]
  transfers between devices with their start and end apart: 5 -> 5, of which waited for: 2 -> 2; matrix products, arithmetic and copies ran while one was open for 1% -> 5% of each run, Pallas kernels for 0% -> 0%
where the time goes in v1:
time: 148 us; the launch traced here: 147 us
  waiting for transfers between devices  92.6 us (63%)
  Pallas kernels  22.2 us (15%)
  between operations  14.8 us (10%)
  local copies, waits for them, and re-layouts  6.01 us (4%)
  matrix products  4.18 us (3%)
  starting transfers between devices  3.72 us (3%)
  other arithmetic  3.39 us (2%)
    psum x1, waiting for transfers between devices, local(): total_gram = lax.psum(local_gram, ('snap', 'slab', 'sub'))  92.5 us
    pallas_call x1, Pallas kernels, local(): pl.pallas_call(functools.partial(whiten_kernel, cells_total), out_shape=(...  22.2 us
    ppermute x2, starting transfers between devices, padded_2(): lax.ppermute(lax.slice_in_dim(block, block.shape[dim] - width, None, axis...  3.53 us
  transfers between devices with their start and end apart: 5, of which 2 were waited for; matrix products, arithmetic and copies ran while one was open for 5% of the time, Pallas kernels for 0%

profile of v1, /device:TPU:0, one launch (start us, length us, event | category | flops | bytes accessed | tf_op | source)
XLA Modules:
  0.0 146.9 jit_solution(15230948213145263411)
XLA Ops:
  7.2 0.0 copy-start.1
  7.2 0.0 all-reduce.2.cloned.1.call-start
  7.2 3.0 %collective-permute-start.1 = (f32[1,4,2,8,128]{4,3,2,1,0:T(8,128)}, f32[1,4,2,8,128]{4,3,2,1,0:T(8,128)S(1)}, u32[]{:S(2)}, u32[]{:S(2)}) collective-permute-start(f32[1,4,2,8,128]{4,3,2,1,0:T(8,128)} %param.5), channel_id=1, source_target_pairs={{0,2},{2,0},{1,3},{3,1},{4,6},{6,4},{5,7},{7,5},{8,10},{10,8},{9,1... | collective-permute-start | bytes 98312 | tf_op jit(solution)/shard_map/ppermute | solution.py:19
  10.3 0.1 collective-permute-start
  10.3 0.9 slice_bitcast_fusion.2
  11.2 0.9 slice_bitcast_fusion.3
  12.1 0.9 slice_bitcast_fusion.6
  13.1 0.9 slice_bitcast_fusion.7
  14.0 0.8 bitcast_dynamic-update-slice_fusion.2
  15.4 1.3 fusion.8
  16.6 0.8 eq.23
  17.4 0.0 collective-permute-done.1
  17.4 0.8 constant_dynamic-update-slice_fusion.1
  18.2 0.0 collective-permute-done
  18.2 0.1 collective-permute-start.2
  18.3 0.5 collective-permute-start.3
  18.8 0.7 bitcast_dynamic-update-slice_fusion.1
  19.5 0.0 collective-permute-done.2
  19.5 0.1 collective-permute-done.3
  19.7 0.1 multiply_dynamic-update-slice_fusion.1
  19.8 0.0 copy-done.1
  19.8 0.1 multiply_dynamic-update-slice_fusion
  20.0 0.0 copy-start.2
  20.0 2.1 %fusion.2 = f32[576,2048]{1,0:T(8,128)S(1)} fusion(f32[28,2048]{1,0:T(8,128)S(1)} %reshape.470, s32[576]{0:T(1024)S(1)} %eq.23), kind=kOutput, calls=%fused_computation.5 | convolution fusion | flops 396377856 | bytes 4950272 | tf_op jit(solution)/shard_map/dot_general | solution.py:36
  22.1 0.0 copy-done.2
  22.1 1.1 fusion.1.feature_ref
  23.2 0.0 copy-start
  23.2 2.1 %fusion.10 = f32[192,192]{1,0:T(8,128)} fusion(f32[192,2048]{1,0:T(8,128)S(1)} %fusion.1.feature_ref), kind=kOutput, calls=%fused_computation.43 | convolution fusion | flops 905969664 | bytes 1720320 | tf_op jit(solution)/shard_map/dot_general | solution.py:125
  25.4 0.0 copy-done
  25.4 0.0 all-reduce.2.cloned.1.call-update
  25.4 92.5 %all-reduce.2.cloned.1.call-done.gram_ref = f32[192,192]{1,0:T(8,128)} async-done(((f32[192,192]{1,0:T(8,128)}), f32[192,192]{1,0:T(8,128)}) %all-reduce.2.cloned.1.call-update) | async-done | bytes 147472 | tf_op jit(solution)/shard_map/psum | solution.py:132
  117.9 22.2 %shard_map.68 = (bf16[1,192,2,8,128]{4,3,2,1,0:T(8,128)(2,1)}, f32[192,192]{1,0:T(8,128)}) custom-call(f32[192,192]{1,0:T(8,128)} %all-reduce.2.cloned.1.call-done.gram_ref, f32[192,2048]{1,0:T(8,128)} %copy-done), custom_call_target="tpu_custom_call" | custom-call | tf_op jit(solution)/shard_map/pallas_call | solution.py:135
  (8 shorter events, 0.1 us)
Async XLA Ops:
  7.2 12.6 %copy-start.1 = (f32[1,4,2,8,128]{4,3,2,1,0:T(8,128)S(1)}, f32[1,4,2,8,128]{4,3,2,1,0:T(8,128)}, u32[]{:S(2)}) copy-start(f32[1,4,2,8,128]{4,3,2,1,0:T(8,128)} %param.5) | copy-start | bytes 98308
  7.2 110.7 %all-reduce.2.cloned.1.call-start = ((), (), s32[]{:S(2)}) async-start(), calls=%async_computation | async-start | bytes 393216 | tf_op jit(solution)/shard_map/psum | solution.py:132
  7.2 10.2 %collective-permute-start.1 = (f32[1,4,2,8,128]{4,3,2,1,0:T(8,128)}, f32[1,4,2,8,128]{4,3,2,1,0:T(8,128)S(1)}, u32[]{:S(2)}, u32[]{:S(2)}) collective-permute-start(f32[1,4,2,8,128]{4,3,2,1,0:T(8,128)} %param.5), channel_id=1, source_target_pairs={{0,2},{2,0},{1,3},{3,1},{4,6},{6,4},{5,7},{7,5},{8,10},{10,8},{9,1... | collective-permute-start | bytes 98312 | tf_op jit(solution)/shard_map/ppermute | solution.py:19
  10.3 7.9 %collective-permute-start = (f32[1,4,2,8,128]{4,3,2,1,0:T(8,128)}, f32[1,4,2,8,128]{4,3,2,1,0:T(8,128)S(1)}, u32[]{:S(2)}, u32[]{:S(2)}) collective-permute-start(f32[1,4,2,8,128]{4,3,2,1,0:T(8,128)} %param.5), channel_id=1, source_target_pairs={{2,0},{0,2},{3,1},{1,3},{6,4},{4,6},{7,5},{5,7},{10,8},{8,10},{11,... | collective-permute-start | bytes 98312 | tf_op jit(solution)/shard_map/ppermute | solution.py:22
  18.2 1.3 collective-permute-start.2
  18.3 1.3 collective-permute-start.3
  20.0 2.1 %copy-start.2 = (f32[192]{0:T(256)S(1)}, f32[192]{0:T(256)}, u32[]{:S(2)}) copy-start(f32[192]{0:T(256)} %param.9) | copy-start | bytes 2308
  23.2 2.1 %copy-start = (f32[192,2048]{1,0:T(8,128)}, f32[192,2048]{1,0:T(8,128)S(1)}, u32[]{:S(2)}) copy-start(f32[192,2048]{1,0:T(8,128)S(1)} %fusion.1.feature_ref) | copy-start | bytes 4718596
Sparse Core Ops, SparseCore 0:
  25.5 92.3 all-reduce.1

commit v2 on v1

v2 whole, which is shorter than its diff:
```python
import functools

import jax
import jax.numpy as jnp
from jax import lax
from jax.experimental import pallas as pl
from jax.experimental.pallas import tpu as pltpu
from jax.sharding import PartitionSpec as P

ridge_value = 0.05
panel_rows = 32
HIGHEST = lax.Precision.HIGHEST
MESH = pl.DeviceIdType.MESH


def eliminate(work, order):
    half = work.shape[1] // 2
    for start in range(0, order, panel_rows):
        stop = start + panel_rows
        low = start // 128 * 128
        high = half + (stop + 127) // 128 * 128
        panel = work[start:stop, low:high]
        row_index = lax.broadcasted_iota(jnp.int32, (panel_rows, 1), 0)
        pivots = jnp.ones((panel_rows, 1), jnp.float32)
        for step in range(panel_rows):
            place = start + step - low
            row = panel[step : step + 1, :]
            pivot = panel[step : step + 1, place : place + 1]
            pivots = jnp.where(row_index == step, pivot, pivots)
            if step + 1 < panel_rows:
                column = panel[:, place : place + 1] * (1.0 / pivot)
                panel = panel - jnp.where(row_index > step, column, 0.0) * row
        panel = panel * (1.0 / jnp.sqrt(pivots))
        work[start:stop, low:high] = panel
        if stop < order:
            sides = panel[:, : half - low].T[stop - low : order - low, :]
            work[stop:order, low:high] = work[stop:order, low:high] - jnp.dot(
                sides, panel, precision=HIGHEST, preferred_element_type=jnp.float32
            )


def whiten_kernel(cells_total, gram_ref, feature_ref, white_ref, factor_ref, work, spread):
    order = gram_ref.shape[0]
    half = work.shape[1] // 2
    rows = lax.broadcasted_iota(jnp.int32, (order, order), 0)
    columns = lax.broadcasted_iota(jnp.int32, (order, order), 1)
    identity = (rows == columns).astype(jnp.float32)
    work[...] = jnp.zeros_like(work)
    work[:, :order] = gram_ref[...] * (1.0 / cells_total) + ridge_value * identity
    work[:, half : half + order] = identity
    eliminate(work, order)
    factor_ref[...] = jnp.where(columns >= rows, work[:, :order], 0.0)
    inverse = jnp.where(columns <= rows, work[:, half : half + order], 0.0)
    tiles = feature_ref.shape[1] // 128
    for tile in range(0, tiles, 2):
        solved = jnp.dot(
            inverse,
            feature_ref[:, tile * 128 : tile * 128 + 256],
            precision=HIGHEST,
            preferred_element_type=jnp.float32,
        )
        spread[pl.ds(tile, order, stride=tiles), :] = solved[:, :128]
        spread[pl.ds(tile + 1, order, stride=tiles), :] = solved[:, 128:]
    white_ref[...] = spread[...].reshape(white_ref.shape).astype(white_ref.dtype)


def plane_device(place, subs):
    return {"slab": lax.div(place, subs), "sub": lax.rem(place, subs)}


def gram_kernel(
    counts,
    fields_ref,
    ids_ref,
    weight_ref,
    terms_ref,
    mix_ref,
    gram_ref,
    feature_ref,
    halo_z,
    halo_x,
    natural,
    partial,
    landed,
    snaps_sum,
    total,
    halo_send,
    halo_recv,
    plane_send,
    plane_recv,
    snap_send,
    snap_recv,
    gather_send,
    gather_recv,
):
    slabs, subs, snaps = counts
    plane = slabs * subs
    slab, sub, snap = lax.axis_index("slab"), lax.axis_index("sub"), lax.axis_index("snap")
    me = slab * subs + sub
    plane_peers = [plane_device(lax.rem(me + k, plane), subs) for k in range(1, plane)]
    snap_peers = [{"snap": lax.rem(snap + k, snaps)} for k in range(1, snaps)]

    barrier = pltpu.get_barrier_semaphore()
    for peer in plane_peers + snap_peers:
        pl.semaphore_signal(barrier, inc=1, device_id=peer, device_id_type=MESH)
    pl.semaphore_wait(barrier, len(plane_peers) + len(snap_peers))

    copies = []
    for axis, index, count, halo, base in (
        ("slab", slab, slabs, halo_z, 0),
        ("sub", sub, subs, halo_x, 2),
    ):
        for side, move in ((0, 1), (1, count - 1))[: 1 if count == 2 else 2]:
            copy = pltpu.make_async_remote_copy(
                src_ref=fields_ref.at[0],
                dst_ref=halo.at[side],
                send_sem=halo_send.at[base + side],
                recv_sem=halo_recv.at[base + side],
                device_id={axis: lax.rem(index + move, count)},
                device_id_type=MESH,
            )
            copy.start()
            copies.append(copy)

    features, terms = terms_ref.shape
    field_count, layers, columns, width = fields_ref.shape[1:]
    cells_rows = layers * columns
    row_of = lax.broadcasted_iota(jnp.int32, (features, 96), 1)
    base_of = lax.rem(row_of, 32)
    chosen = [
        (terms_ref[:, k : k + 1] == base_of).astype(jnp.float32).astype(jnp.bfloat16)
        for k in range(3)
    ]
    choose = jnp.concatenate(chosen, axis=0)
    table = lax.broadcasted_iota(jnp.int32, weight_ref.shape, 1)
    scale = jnp.sum(
        jnp.where(table == ids_ref[0], weight_ref[...], 0.0), axis=1, keepdims=True
    )
    square_rows = lax.broadcasted_iota(jnp.int32, (features, features), 0)
    square_columns = lax.broadcasted_iota(jnp.int32, (features, features), 1)
    mix = jnp.sum(
        jnp.where(square_rows == square_columns, mix_ref[...], 0.0), axis=1, keepdims=True
    )
    natural[28 * cells_rows :, :] = jnp.zeros((4 * cells_rows, width), jnp.float32)

    def put(field, kind, layer, tile):
        start = (field * 7 + kind) * cells_rows + layer * columns
        natural[start : start + columns, :] = tile

    def pair(center, ahead_one, behind_one, ahead_two, behind_two):
        first = 8.0 * (ahead_one - behind_one) - (ahead_two - behind_two)
        second = 16.0 * (ahead_one + behind_one) - (ahead_two + behind_two) - 30.0 * center
        return first * (1.0 / 12.0), second * (1.0 / 12.0)

    for f in range(field_count):
        for z in range(layers):
            tile = fields_ref[0, f, z]
            put(f, 0, z, tile)
            y_shifts = [pltpu.roll(tile, s % width, 1) for s in (-1, 1, -2, 2)]
            first, second = pair(tile, *y_shifts)
            put(f, 3, z, first)
            put(f, 6, z, second)

    for copy in copies:
        copy.wait()

    z_low, z_high = 0, 0 if slabs == 2 else 1
    x_low, x_high = 0, 0 if subs == 2 else 1
    line = lax.broadcasted_iota(jnp.int32, (columns, width), 0)
    for f in range(field_count):
        column = [halo_z[z_low, f, z] for z in range(layers)]
        column += [fields_ref[0, f, z] for z in range(layers)]
        column += [halo_z[z_high, f, z] for z in range(layers)]
        for z in range(layers):
            tile = column[layers + z]
            at = layers + z
            first, second = pair(
                tile, column[at + 1], column[at - 1], column[at + 2], column[at - 2]
            )
            put(f, 1, z, first)
            put(f, 4, z, second)
            low, high = halo_x[x_low, f, z], halo_x[x_high, f, z]
            shifts = []
            for s in (-1, 1, -2, 2):
                turned = pltpu.roll(tile, s % columns, 0)
                other = pltpu.roll(high if s < 0 else low, s % columns, 0)
                inside = line < columns + s if s < 0 else line >= s
                shifts.append(jnp.where(inside, turned, other))
            first, second = pair(tile, *shifts)
            put(f, 2, z, first)
            put(f, 5, z, second)

    for start in range(0, cells_rows, 2):
        pieces = []
        for at in (start, start + 1):
            whole = natural[pl.ds(at, 32, stride=cells_rows), :]
            upper = whole.astype(jnp.bfloat16)
            rest = whole - upper.astype(jnp.float32)
            centre = rest.astype(jnp.bfloat16)
            lower = (rest - centre.astype(jnp.float32)).astype(jnp.bfloat16)
            pieces.append(jnp.concatenate([upper, centre, lower], axis=0))
        picked = jnp.dot(
            choose, jnp.concatenate(pieces, axis=1), preferred_element_type=jnp.float32
        )
        left, middle = picked[:features], picked[features : 2 * features]
        right = picked[2 * features :]
        feature_ref[:, start * width : (start + 2) * width] = (
            scale * left * (middle + mix * right)
        )

    everything = feature_ref[...]
    gram = lax.dot_general(
        everything,
        everything,
        (((1,), (1,)), ((), ())),
        precision=HIGHEST,
        preferred_element_type=jnp.float32,
    )
    rows = features // plane
    for k in range(plane):
        partial[k] = gram[k * rows : (k + 1) * rows, :]

    copies = []
    for k in range(1, plane):
        copy = pltpu.make_async_remote_copy(
            src_ref=partial.at[lax.rem(me + k, plane)],
            dst_ref=landed.at[k - 1],
            send_sem=plane_send.at[k - 1],
            recv_sem=plane_recv.at[k - 1],
            device_id=plane_peers[k - 1],
            device_id_type=MESH,
        )
        copy.start()
        copies.append(copy)
    block = partial[me]
    for k in range(1, plane):
        copies[k - 1].wait()
        block = block + landed[k - 1]
    snaps_sum[snap] = block

    copies = []
    for k in range(1, snaps):
        copy = pltpu.make_async_remote_copy(
            src_ref=snaps_sum.at[snap],
            dst_ref=snaps_sum.at[snap],
            send_sem=snap_send.at[k - 1],
            recv_sem=snap_recv.at[k - 1],
            device_id=snap_peers[k - 1],
            device_id_type=MESH,
        )
        copy.start()
        copies.append(copy)
    for copy in copies:
        copy.wait()
    block = snaps_sum[0]
    for k in range(1, snaps):
        block = block + snaps_sum[k]
    total[me] = block

    copies = []
    for k in range(1, plane):
        copy = pltpu.make_async_remote_copy(
            src_ref=total.at[me],
            dst_ref=total.at[me],
            send_sem=gather_send.at[k - 1],
            recv_sem=gather_recv.at[k - 1],
            device_id=plane_peers[k - 1],
            device_id_type=MESH,
        )
        copy.start()
        copies.append(copy)
    for copy in copies:
        copy.wait()
    for k in range(plane):
        gram_ref[k * rows : (k + 1) * rows, :] = total[k]


def local(fields, snap_ids, snap_weight, product_terms, mix_weight):
    counts = tuple(lax.axis_size(axis) for axis in ("slab", "sub", "snap"))
    slabs, subs, snaps = counts
    plane = slabs * subs
    field_count, layers, columns, width = fields.shape[1:]
    features = product_terms.shape[0]
    cells = layers * columns * width
    rows = features // plane
    f32 = jnp.float32
    in_vmem = pl.BlockSpec(memory_space=pltpu.VMEM)
    total_gram, values = pl.pallas_call(
        functools.partial(gram_kernel, counts),
        out_shape=(
            jax.ShapeDtypeStruct((features, features), f32),
            jax.ShapeDtypeStruct((features, cells), f32),
        ),
        in_specs=[in_vmem, pl.BlockSpec(memory_space=pltpu.SMEM), in_vmem, in_vmem, in_vmem],
        out_specs=(in_vmem, in_vmem),
        scratch_shapes=[
            pltpu.VMEM((2,) + fields.shape[1:], f32),
            pltpu.VMEM((2,) + fields.shape[1:], f32),
            pltpu.VMEM((32 * layers * columns, width), f32),
            pltpu.VMEM((plane, rows, features), f32),
            pltpu.VMEM((plane - 1, rows, features), f32),
            pltpu.VMEM((snaps, rows, features), f32),
            pltpu.VMEM((plane, rows, features), f32),
            pltpu.SemaphoreType.DMA((4,)),
            pltpu.SemaphoreType.DMA((4,)),
            pltpu.SemaphoreType.DMA((plane - 1,)),
            pltpu.SemaphoreType.DMA((plane - 1,)),
            pltpu.SemaphoreType.DMA((snaps - 1,)),
            pltpu.SemaphoreType.DMA((snaps - 1,)),
            pltpu.SemaphoreType.DMA((plane - 1,)),
            pltpu.SemaphoreType.DMA((plane - 1,)),
        ],
        compiler_params=pltpu.CompilerParams(collective_id=0, has_side_effects=True),
    )(fields, snap_ids, snap_weight.reshape(1, -1), product_terms, mix_weight.reshape(1, -1))
    whitened, r_factor = pl.pallas_call(
        functools.partial(whiten_kernel, float(snaps * plane * cells)),
        out_shape=(
            jax.ShapeDtypeStruct((1, features, layers, columns, width), jnp.bfloat16),
            jax.ShapeDtypeStruct((features, features), f32),
        ),
        in_specs=[in_vmem, in_vmem],
        out_specs=(in_vmem, in_vmem),
        scratch_shapes=[
            pltpu.VMEM((features, 512), f32),
            pltpu.VMEM((features * (cells // 128), 128), f32),
        ],
    )(total_gram, values)
    return (whitened, r_factor)


def solution(mesh):
    return jax.shard_map(
        local,
        mesh=mesh,
        in_specs=(
            P(("groups", "snap"), None, "slab", "sub", None),
            P(("groups", "snap")),
            P(),
            P(),
            P(),
        ),
        out_specs=(P(("groups", "snap"), None, "slab", "sub", None), P("groups", None)),
        check_vma=False,
    )
```

time: 148 us -> 50.1 us (0.34)
  waiting for transfers between devices: 92.6 us -> 0 us
  Pallas kernels: 22.2 us -> 47.2 us
  between operations: 14.8 us -> 1.28 us
  local copies, waits for them, and re-layouts: 6.01 us -> 1.45 us
  matrix products: 4.18 us -> 0 us
  starting transfers between devices: 3.72 us -> 0 us
  other arithmetic: 3.39 us -> 0 us
    psum x1 -> x0, waiting for transfers between devices: 92.5 us -> none  [local(): total_gram = lax.psum(local_gram, ('snap', 'slab', 'sub'))]
    pallas_call x1 -> x2, Pallas kernels: 22.2 us -> 47.2 us  [the longest x1 25 us: local(): pl.pallas_call(functools.partial(gram_kernel, counts), out_shape=(jax.Sha...]
    dot_general x2 -> x0, matrix products: 4.18 us -> none  [the longest x1 2.11 us: local(): lax.dot_general(features, features, (((1,), (1,)), ((), ())), precision=H...]
    ppermute x4 -> x0, starting transfers between devices: 3.68 us -> none  [the longest x2 3.53 us: padded_2(): lax.ppermute(lax.slice_in_dim(block, block.shape[dim] - width, None, axis...]
    concatenate x5 -> x0, local copies, waits for them, and re-layouts: 3.63 us -> none  [the longest x2 1.82 us: local(): jnp.roll(center, -1, 3)]
  transfers between devices with their start and end apart: 5 -> 0, of which waited for: 2 -> 0; matrix products, arithmetic and copies ran while one was open for 5% -> 0% of each run, Pallas kernels for 0% -> 0%
where the time goes in v2:
time: 50.1 us; the launch traced here: 49.9 us
  Pallas kernels  47.2 us (94%)
  local copies, waits for them, and re-layouts  1.45 us (3%)
  between operations  1.28 us (3%)
    pallas_call x1, Pallas kernels, local(): pl.pallas_call(functools.partial(gram_kernel, counts), out_shape=(jax.Sha...  25 us
    pallas_call x1, Pallas kernels, local(): pl.pallas_call(functools.partial(whiten_kernel, float(snaps * plane * cel...  22.2 us
    unnamed x1, local copies, waits for them, and re-layouts  1.45 us

profile of v2, /device:TPU:0, one launch (start us, length us, event | category | flops | bytes accessed | tf_op | source)
XLA Modules:
  0.0 49.9 jit_solution(5281040534529145712)
XLA Ops:
  1.3 1.4 %copy.7.terms_ref = s32[192,3]{1,0:T(8,128)} copy(s32[192,3]{0,1:T(4,128)} %param.8) | data formatting | bytes 4608 | tf_op args[3]
  2.7 25.0 %shard_map.68 = (f32[192,192]{1,0:T(8,128)}, f32[192,2048]{1,0:T(8,128)}) custom-call(f32[1,4,2,8,128]{4,3,2,1,0:T(8,128)} %fields_ref.1, s32[1]{0:T(128)S(6)} %copy.8.ids_ref, f32[1,64]{1,0:T(1,128)} %bitcast.3, s32[192,3]{1,0:T(8,128)} %copy.7.terms_ref, f32[1,192]{1,0:T(1,128)} %bitcast.2), custom_call_target="tpu_custom_call" | custom-call | tf_op jit(solution)/shard_map/pallas_call | solution.py:288
  27.7 22.2 %shard_map.69 = (bf16[1,192,2,8,128]{4,3,2,1,0:T(8,128)(2,1)}, f32[192,192]{1,0:T(8,128)}) custom-call(f32[192,192]{1,0:T(8,128)} %get-tuple-element.4.gram_ref, f32[192,2048]{1,0:T(8,128)} %get-tuple-element.5.feature_ref), custom_call_target="tpu_custom_call" | custom-call | tf_op jit(solution)/shard_map/pallas_call | solution.py:315

commit v3 on v2

--- a/solution.py
+++ b/solution.py
@@ -13,51 +13,126 @@
 MESH = pl.DeviceIdType.MESH
 
 
+def split(values, count):
+    parts = []
+    for _ in range(count):
+        part = values.astype(jnp.bfloat16)
+        parts.append(part)
+        values = values - part.astype(jnp.float32)
+    return parts
+
+
+def row_of(tile, place):
+    return jnp.broadcast_to(tile[place : place + 1, :], tile.shape)
+
+
+def eliminate_group(groups, first, place):
+    line = lax.broadcasted_iota(jnp.int32, (8, 128), 0)
+    lane_tile, lane = place // 128, place % 128
+    later = range(first, len(groups))
+    spread = {
+        (r, c): jnp.broadcast_to(
+            groups[r][lane_tile][:, lane + c : lane + c + 1], (8, 128)
+        )
+        for r in later
+        for c in range(8)
+    }
+    pivots = jnp.ones((8, 128), jnp.float32)
+    factors = []
+    for j in range(8):
+        pivot = row_of(spread[first, j], j)
+        pivots = jnp.where(line == j, pivot, pivots)
+        inverse = 1.0 / pivot
+        scaled = {r: spread[r, j] * inverse for r in later}
+        scaled[first] = jnp.where(line > j, scaled[first], 0.0)
+        factors.append(scaled)
+        for c in range(j + 1, 8):
+            head = row_of(spread[first, c], j)
+            for r in later:
+                spread[r, c] = spread[r, c] - scaled[r] * head
+    for t in range(len(groups[first])):
+        tile = groups[first][t]
+        for j in range(8):
+            head = row_of(tile, j)
+            if j < 7:
+                tile = tile - factors[j][first] * head
+            for r in later:
+                if r > first:
+                    groups[r][t] = groups[r][t] - factors[j][r] * head
+        groups[first][t] = tile
+    return 1.0 / jnp.sqrt(pivots)
+
+
 def eliminate(work, order):
     half = work.shape[1] // 2
     for start in range(0, order, panel_rows):
         stop = start + panel_rows
         low = start // 128 * 128
         high = half + (stop + 127) // 128 * 128
-        panel = work[start:stop, low:high]
-        row_index = lax.broadcasted_iota(jnp.int32, (panel_rows, 1), 0)
-        pivots = jnp.ones((panel_rows, 1), jnp.float32)
-        for step in range(panel_rows):
-            place = start + step - low
-            row = panel[step : step + 1, :]
-            pivot = panel[step : step + 1, place : place + 1]
-            pivots = jnp.where(row_index == step, pivot, pivots)
-            if step + 1 < panel_rows:
-                column = panel[:, place : place + 1] * (1.0 / pivot)
-                panel = panel - jnp.where(row_index > step, column, 0.0) * row
-        panel = panel * (1.0 / jnp.sqrt(pivots))
+        tiles = (high - low) // 128
+        groups = [
+            [work[r : r + 8, low + 128 * t : low + 128 * t + 128] for t in range(tiles)]
+            for r in range(start, stop, 8)
+        ]
+        scales = [
+            eliminate_group(groups, g, start + 8 * g - low) for g in range(panel_rows // 8)
+        ]
+        rows = [
+            jnp.concatenate([tile * scale for tile in group], axis=1)
+            for group, scale in zip(groups, scales)
+        ]
+        panel = jnp.concatenate(rows, axis=0)
         work[start:stop, low:high] = panel
         if stop < order:
             sides = panel[:, : half - low].T[stop - low : order - low, :]
+            a, b, c = split(sides, 3)
+            d, e, f = split(panel, 3)
+            left = jnp.concatenate([a, a, b, b, a, c], axis=1)
+            right = jnp.concatenate([d, e, d, e, f, d], axis=0)
             work[stop:order, low:high] = work[stop:order, low:high] - jnp.dot(
-                sides, panel, precision=HIGHEST, preferred_element_type=jnp.float32
+                left, right, preferred_element_type=jnp.float32
             )
 
 
-def whiten_kernel(cells_total, gram_ref, feature_ref, white_ref, factor_ref, work, spread):
-    order = gram_ref.shape[0]
+def whiten_kernel(
+    cells_total, packed_ref, feature_in, white_ref, factor_ref, work, spread, feature_ref, done
+):
+    feature_copy = pltpu.make_async_copy(feature_in, feature_ref, done)
+    feature_copy.start()
+    order = factor_ref.shape[0]
+    middle = packed_ref.shape[0]
     half = work.shape[1] // 2
     rows = lax.broadcasted_iota(jnp.int32, (order, order), 0)
     columns = lax.broadcasted_iota(jnp.int32, (order, order), 1)
-    identity = (rows == columns).astype(jnp.float32)
-    work[...] = jnp.zeros_like(work)
-    work[:, :order] = gram_ref[...] * (1.0 / cells_total) + ridge_value * identity
-    work[:, half : half + order] = identity
+    row = lax.broadcasted_iota(jnp.int32, (middle, 128), 0)
+    lane = lax.broadcasted_iota(jnp.int32, (middle, 128), 1)
+    left = packed_ref[:, :128]
+    turned = jnp.concatenate([left, jnp.zeros((128 - middle, 128), jnp.float32)], axis=0).T
+    turned = turned[:middle, :]
+    work[:middle, :128] = jnp.where((lane >= row) | (lane >= middle), left, turned)
+    work[:middle, 128:half] = jnp.where(lane + 128 < order, packed_ref[:, 128:], 0.0)
+    corner = packed_ref[:, order : order + 1]
+    lower = jnp.where(lane < row, left, jnp.where(lane > row, turned, corner))
+    lower = jnp.where(lane < middle, lower, 0.0)
+    lower = jnp.concatenate([lower, jnp.zeros((middle, half - 128), jnp.float32)], axis=1)
+    work[middle:, :half] = pltpu.roll(lower, middle, 1)
+    long_rows = lax.broadcasted_iota(jnp.int32, (order, half), 0)
+    long_columns = lax.broadcasted_iota(jnp.int32, (order, half), 1)
+    identity = (long_rows == long_columns).astype(jnp.float32)
+    work[:, half:] = identity
+    work[:, :half] = work[:, :half] * (1.0 / cells_total) + ridge_value * identity
     eliminate(work, order)
     factor_ref[...] = jnp.where(columns >= rows, work[:, :order], 0.0)
     inverse = jnp.where(columns <= rows, work[:, half : half + order], 0.0)
+    upper, lower = split(inverse, 2)
+    feature_copy.wait()
     tiles = feature_ref.shape[1] // 128
     for tile in range(0, tiles, 2):
-        solved = jnp.dot(
-            inverse,
-            feature_ref[:, tile * 128 : tile * 128 + 256],
-            precision=HIGHEST,
-            preferred_element_type=jnp.float32,
+        first, second = split(feature_ref[:, tile * 128 : tile * 128 + 256], 2)
+        solved = (
+            jnp.dot(upper, first, preferred_element_type=jnp.float32)
+            + jnp.dot(upper, second, preferred_element_type=jnp.float32)
+            + jnp.dot(lower, first, preferred_element_type=jnp.float32)
         )
         spread[pl.ds(tile, order, stride=tiles), :] = solved[:, :128]
         spread[pl.ds(tile + 1, order, stride=tiles), :] = solved[:, 128:]
@@ -75,8 +150,11 @@
     weight_ref,
     terms_ref,
     mix_ref,
-    gram_ref,
+    packed_ref,
+    feature_out,
     feature_ref,
+    gram_wide,
+    feature_done,
     halo_z,
     halo_x,
     natural,
@@ -103,6 +181,49 @@
     barrier = pltpu.get_barrier_semaphore()
     for peer in plane_peers + snap_peers:
         pl.semaphore_signal(barrier, inc=1, device_id=peer, device_id_type=MESH)
+    features = terms_ref.shape[1]
+    field_count, layers, columns, width = fields_ref.shape[1:]
+    cells_rows = layers * columns
+    square_rows = lax.broadcasted_iota(jnp.int32, (features, features), 0)
+    square_columns = lax.broadcasted_iota(jnp.int32, (features, features), 1)
+
+    def upright(row):
+        return jnp.sum(jnp.where(square_rows == square_columns, row, 0.0), axis=1, keepdims=True)
+
+    slot = lax.broadcasted_iota(jnp.int32, (features, 96), 1)
+    base_of = lax.rem(slot, 32).astype(jnp.float32)
+    chosen = [
+        (upright(terms_ref[k : k + 1, :].astype(jnp.float32)) == base_of)
+        .astype(jnp.float32)
+        .astype(jnp.bfloat16)
+        for k in range(3)
+    ]
+    choose = jnp.concatenate(chosen, axis=0)
+    mix = upright(mix_ref[...])
+    table = lax.broadcasted_iota(jnp.int32, weight_ref.shape, 1)
+    scale = jnp.sum(
+        jnp.where(table == ids_ref[0], weight_ref[...], 0.0), axis=1, keepdims=True
+    )
+    natural[28 * cells_rows :, :] = jnp.zeros((4 * cells_rows, width), jnp.float32)
+
+    def put(field, kind, layer, tile):
+        start = (field * 7 + kind) * cells_rows + layer * columns
+        natural[start : start + columns, :] = tile
+
+    def pair(center, ahead_one, behind_one, ahead_two, behind_two):
+        first = 8.0 * (ahead_one - behind_one) - (ahead_two - behind_two)
+        second = 16.0 * (ahead_one + behind_one) - (ahead_two + behind_two) - 30.0 * center
+        return first * (1.0 / 12.0), second * (1.0 / 12.0)
+
+    for f in range(field_count):
+        for z in range(layers):
+            tile = fields_ref[0, f, z]
+            put(f, 0, z, tile)
+            y_shifts = [pltpu.roll(tile, s % width, 1) for s in (-1, 1, -2, 2)]
+            first, second = pair(tile, *y_shifts)
+            put(f, 3, z, first)
+            put(f, 6, z, second)
+
     pl.semaphore_wait(barrier, len(plane_peers) + len(snap_peers))
 
     copies = []
@@ -121,45 +242,6 @@
             )
             copy.start()
             copies.append(copy)
-
-    features, terms = terms_ref.shape
-    field_count, layers, columns, width = fields_ref.shape[1:]
-    cells_rows = layers * columns
-    row_of = lax.broadcasted_iota(jnp.int32, (features, 96), 1)
-    base_of = lax.rem(row_of, 32)
-    chosen = [
-        (terms_ref[:, k : k + 1] == base_of).astype(jnp.float32).astype(jnp.bfloat16)
-        for k in range(3)
-    ]
-    choose = jnp.concatenate(chosen, axis=0)
-    table = lax.broadcasted_iota(jnp.int32, weight_ref.shape, 1)
-    scale = jnp.sum(
-        jnp.where(table == ids_ref[0], weight_ref[...], 0.0), axis=1, keepdims=True
-    )
-    square_rows = lax.broadcasted_iota(jnp.int32, (features, features), 0)
-    square_columns = lax.broadcasted_iota(jnp.int32, (features, features), 1)
-    mix = jnp.sum(
-        jnp.where(square_rows == square_columns, mix_ref[...], 0.0), axis=1, keepdims=True
-    )
-    natural[28 * cells_rows :, :] = jnp.zeros((4 * cells_rows, width), jnp.float32)
-
-    def put(field, kind, layer, tile):
-        start = (field * 7 + kind) * cells_rows + layer * columns
-        natural[start : start + columns, :] = tile
-
-    def pair(center, ahead_one, behind_one, ahead_two, behind_two):
-        first = 8.0 * (ahead_one - behind_one) - (ahead_two - behind_two)
-        second = 16.0 * (ahead_one + behind_one) - (ahead_two + behind_two) - 30.0 * center
-        return first * (1.0 / 12.0), second * (1.0 / 12.0)
-
-    for f in range(field_count):
-        for z in range(layers):
-            tile = fields_ref[0, f, z]
-            put(f, 0, z, tile)
-            y_shifts = [pltpu.roll(tile, s % width, 1) for s in (-1, 1, -2, 2)]
-            first, second = pair(tile, *y_shifts)
-            put(f, 3, z, first)
-            put(f, 6, z, second)
 
     for copy in copies:
         copy.wait()
@@ -208,17 +290,31 @@
             scale * left * (middle + mix * right)
         )
 
+    feature_copy = pltpu.make_async_copy(feature_ref, feature_out, feature_done)
+    feature_copy.start()
     everything = feature_ref[...]
-    gram = lax.dot_general(
+    wide = gram_wide.shape[1]
+    gram_wide[:, :features] = lax.dot_general(
         everything,
         everything,
         (((1,), (1,)), ((), ())),
         precision=HIGHEST,
         preferred_element_type=jnp.float32,
     )
-    rows = features // plane
+    half = features // 2
+    above = gram_wide[:half, :]
+    below = gram_wide[half:, :]
+    row = lax.broadcasted_iota(jnp.int32, (half, wide), 0)
+    lane = lax.broadcasted_iota(jnp.int32, (half, wide), 1)
+    corner = jnp.sum(jnp.where(lane == row + half, below, 0.0), axis=1, keepdims=True)
+    packed = jnp.where(
+        lane < half,
+        jnp.where(lane >= row, above, pltpu.roll(below, wide - half, 1)),
+        jnp.where(lane < features, above, corner),
+    )
+    rows = half // plane
     for k in range(plane):
-        partial[k] = gram[k * rows : (k + 1) * rows, :]
+        partial[k] = packed[k * rows : (k + 1) * rows, :]
 
     copies = []
     for k in range(1, plane):
@@ -272,7 +368,8 @@
     for copy in copies:
         copy.wait()
     for k in range(plane):
-        gram_ref[k * rows : (k + 1) * rows, :] = total[k]
+        packed_ref[k * rows : (k + 1) * rows, :] = total[k]
+    feature_copy.wait()
 
 
 def local(fields, snap_ids, snap_weight, product_terms, mix_weight):
@@ -282,25 +379,30 @@
     field_count, layers, columns, width = fields.shape[1:]
     features = product_terms.shape[0]
     cells = layers * columns * width
-    rows = features // plane
+    half = features // 2
+    rows = half // plane
+    wide = features // 128 * 128 + 128
     f32 = jnp.float32
     in_vmem = pl.BlockSpec(memory_space=pltpu.VMEM)
     total_gram, values = pl.pallas_call(
         functools.partial(gram_kernel, counts),
         out_shape=(
-            jax.ShapeDtypeStruct((features, features), f32),
+            jax.ShapeDtypeStruct((half, wide), f32),
             jax.ShapeDtypeStruct((features, cells), f32),
         ),
         in_specs=[in_vmem, pl.BlockSpec(memory_space=pltpu.SMEM), in_vmem, in_vmem, in_vmem],
-        out_specs=(in_vmem, in_vmem),
+        out_specs=(in_vmem, pl.BlockSpec(memory_space=pl.ANY)),
         scratch_shapes=[
+            pltpu.VMEM((features, cells), f32),
+            pltpu.VMEM((features, wide), f32),
+            pltpu.SemaphoreType.DMA,
             pltpu.VMEM((2,) + fields.shape[1:], f32),
             pltpu.VMEM((2,) + fields.shape[1:], f32),
             pltpu.VMEM((32 * layers * columns, width), f32),
-            pltpu.VMEM((plane, rows, features), f32),
-            pltpu.VMEM((plane - 1, rows, features), f32),
-            pltpu.VMEM((snaps, rows, features), f32),
-            pltpu.VMEM((plane, rows, features), f32),
+            pltpu.VMEM((plane, rows, wide), f32),
+            pltpu.VMEM((plane - 1, rows, wide), f32),
+            pltpu.VMEM((snaps, rows, wide), f32),
+            pltpu.VMEM((plane, rows, wide), f32),
             pltpu.SemaphoreType.DMA((4,)),
             pltpu.SemaphoreType.DMA((4,)),
             pltpu.SemaphoreType.DMA((plane - 1,)),
@@ -311,18 +413,20 @@
             pltpu.SemaphoreType.DMA((plane - 1,)),
         ],
         compiler_params=pltpu.CompilerParams(collective_id=0, has_side_effects=True),
-    )(fields, snap_ids, snap_weight.reshape(1, -1), product_terms, mix_weight.reshape(1, -1))
+    )(fields, snap_ids, snap_weight.reshape(1, -1), product_terms.T, mix_weight.reshape(1, -1))
     whitened, r_factor = pl.pallas_call(
         functools.partial(whiten_kernel, float(snaps * plane * cells)),
         out_shape=(
             jax.ShapeDtypeStruct((1, features, layers, columns, width), jnp.bfloat16),
             jax.ShapeDtypeStruct((features, features), f32),
         ),
-        in_specs=[in_vmem, in_vmem],
+        in_specs=[in_vmem, pl.BlockSpec(memory_space=pl.ANY)],
         out_specs=(in_vmem, in_vmem),
         scratch_shapes=[
-            pltpu.VMEM((features, 512), f32),
+            pltpu.VMEM((features, 2 * wide), f32),
             pltpu.VMEM((features * (cells // 128), 128), f32),
+            pltpu.VMEM((features, cells), f32),
+            pltpu.SemaphoreType.DMA,
         ],
     )(total_gram, values)
     return (whitened, r_factor)

time: 50.1 us -> 33.8 us (0.67)
  Pallas kernels: 47.2 us -> 32.2 us
  local copies, waits for them, and re-layouts: 1.45 us -> 0 us
    pallas_call x1, Pallas kernels: 22.2 us -> 10.5 us  [local(): pl.pallas_call(functools.partial(whiten_kernel, float(snaps * plane * cel...]
    pallas_call x1, Pallas kernels: 25 us -> 21.7 us  [local(): pl.pallas_call(functools.partial(gram_kernel, counts), out_shape=(jax.Sha...]
    unnamed x1 -> x0, local copies, waits for them, and re-layouts: 1.45 us -> none
where the time goes in v3:
time: 33.8 us; the launch traced here: 33.5 us
  Pallas kernels  32.2 us (95%)
  between operations  1.28 us (4%)
    pallas_call x1, Pallas kernels, local(): pl.pallas_call(functools.partial(gram_kernel, counts), out_shape=(jax.Sha...  21.7 us
    pallas_call x1, Pallas kernels, local(): pl.pallas_call(functools.partial(whiten_kernel, float(snaps * plane * cel...  10.5 us

profile of v3, /device:TPU:0, one launch (start us, length us, event | category | flops | bytes accessed | tf_op | source)
XLA Modules:
  0.0 33.5 jit_solution(10653167170450950311)
XLA Ops:
  1.3 21.7 %shard_map.68 = (f32[96,256]{1,0:T(8,128)}, f32[192,2048]{1,0:T(8,128)}) custom-call(f32[1,4,2,8,128]{4,3,2,1,0:T(8,128)} %fields_ref.1, s32[1]{0:T(128)S(6)} %copy.7.ids_ref, f32[1,64]{1,0:T(1,128)} %bitcast.5, s32[3,192]{1,0:T(4,128)} %bitcast.3, f32[1,192]{1,0:T(1,128)} %bitcast.4), custom_call_target="tpu_custom_call" | custom-call | tf_op jit(solution)/shard_map/pallas_call | solution.py:387
  23.0 10.5 %shard_map.69 = (bf16[1,192,2,8,128]{4,3,2,1,0:T(8,128)(2,1)}, f32[192,192]{1,0:T(8,128)}) custom-call(f32[96,256]{1,0:T(8,128)} %get-tuple-element.4.packed_ref, f32[192,2048]{1,0:T(8,128)} %get-tuple-element.5.feature_in), custom_call_target="tpu_custom_call" | custom-call | tf_op jit(solution)/shard_map/pallas_call | solution.py:417

commit v4 on v3

--- a/solution.py
+++ b/solution.py
@@ -145,13 +145,18 @@
 
 def gram_kernel(
     counts,
+    fields_in,
+    ids_ref,
+    weight_in,
+    terms_in,
+    mix_in,
+    packed_ref,
+    feature_out,
     fields_ref,
-    ids_ref,
     weight_ref,
     terms_ref,
     mix_ref,
-    packed_ref,
-    feature_out,
+    load_done,
     feature_ref,
     gram_wide,
     feature_done,
@@ -178,9 +183,24 @@
     plane_peers = [plane_device(lax.rem(me + k, plane), subs) for k in range(1, plane)]
     snap_peers = [{"snap": lax.rem(snap + k, snaps)} for k in range(1, snaps)]
 
+    loads = [
+        pltpu.make_async_copy(source, target, load_done.at[k])
+        for k, (source, target) in enumerate(
+            (
+                (fields_in, fields_ref),
+                (terms_in, terms_ref),
+                (mix_in, mix_ref),
+                (weight_in, weight_ref),
+            )
+        )
+    ]
+    for load in loads:
+        load.start()
     barrier = pltpu.get_barrier_semaphore()
     for peer in plane_peers + snap_peers:
         pl.semaphore_signal(barrier, inc=1, device_id=peer, device_id_type=MESH)
+    for load in loads:
+        load.wait()
     features = terms_ref.shape[1]
     field_count, layers, columns, width = fields_ref.shape[1:]
     cells_rows = layers * columns
@@ -384,15 +404,21 @@
     wide = features // 128 * 128 + 128
     f32 = jnp.float32
     in_vmem = pl.BlockSpec(memory_space=pltpu.VMEM)
+    anywhere = pl.BlockSpec(memory_space=pl.ANY)
     total_gram, values = pl.pallas_call(
         functools.partial(gram_kernel, counts),
         out_shape=(
-            jax.ShapeDtypeStruct((half, wide), f32),
+            pltpu.VMEM((half, wide), f32),
             jax.ShapeDtypeStruct((features, cells), f32),
         ),
-        in_specs=[in_vmem, pl.BlockSpec(memory_space=pltpu.SMEM), in_vmem, in_vmem, in_vmem],
+        in_specs=[anywhere, pl.BlockSpec(memory_space=pltpu.SMEM)] + [anywhere] * 3,
         out_specs=(in_vmem, pl.BlockSpec(memory_space=pl.ANY)),
         scratch_shapes=[
+            pltpu.VMEM(fields.shape, f32),
+            pltpu.VMEM((1, snap_weight.shape[0]), f32),
+            pltpu.VMEM((3, features), jnp.int32),
+            pltpu.VMEM((1, features), f32),
+            pltpu.SemaphoreType.DMA((4,)),
             pltpu.VMEM((features, cells), f32),
             pltpu.VMEM((features, wide), f32),
             pltpu.SemaphoreType.DMA,
@@ -428,7 +454,8 @@
             pltpu.VMEM((features, cells), f32),
             pltpu.SemaphoreType.DMA,
         ],
-    )(total_gram, values)
+        compiler_params=pltpu.CompilerParams(vmem_limit_bytes=24 * 1024 * 1024),
+    )(pltpu.with_memory_space_constraint(total_gram, pltpu.VMEM), values)
     return (whitened, r_factor)
 
 

time: 33.8 us -> 32.2 us (0.953)
  Pallas kernels: 32.2 us -> 29.3 us
  local copies, waits for them, and re-layouts: 0 us -> 1.4 us
    pallas_call x1, Pallas kernels: 10.5 us -> 8.65 us  [local(): pl.pallas_call(functools.partial(whiten_kernel, float(snaps * plane * cel...]
    unnamed x0 -> x2, local copies, waits for them, and re-layouts: none -> 1.4 us
    pallas_call x1, Pallas kernels: 21.7 us -> 20.7 us  [local(): pl.pallas_call(functools.partial(gram_kernel, counts), out_shape=(pltpu.V...]
where the time goes in v4:
time: 32.2 us; the launch traced here: 32 us
  Pallas kernels  29.3 us (91%)
  local copies, waits for them, and re-layouts  1.4 us (4%)
  between operations  1.29 us (4%)
    pallas_call x1, Pallas kernels, local(): pl.pallas_call(functools.partial(gram_kernel, counts), out_shape=(pltpu.V...  20.7 us
    pallas_call x1, Pallas kernels, local(): pl.pallas_call(functools.partial(whiten_kernel, float(snaps * plane * cel...  8.65 us
    unnamed x2, local copies, waits for them, and re-layouts  1.4 us

profile of v4, /device:TPU:0, one launch (start us, length us, event | category | flops | bytes accessed | tf_op | source)
XLA Modules:
  0.0 32.0 jit_solution(9390324799557688005)
XLA Ops:
  1.3 20.7 %shard_map.68 = (f32[96,256]{1,0:T(8,128)S(1)}, f32[192,2048]{1,0:T(8,128)}) custom-call(f32[1,4,2,8,128]{4,3,2,1,0:T(8,128)} %fields_in.1, s32[1]{0:T(128)S(6)} %copy.7.ids_ref, f32[1,64]{1,0:T(1,128)} %bitcast.5, s32[3,192]{1,0:T(4,128)} %bitcast.3, f32[1,192]{1,0:T(1,128)} %bitcast.4), custom_call_target="tpu_custom_call" | custom-call | tf_op jit(solution)/shard_map/pallas_call | solution.py:408
  22.0 0.0 copy-start
  22.0 1.4 %copy-done = f32[192,2048]{1,0:T(8,128)S(1)} copy-done((f32[192,2048]{1,0:T(8,128)S(1)}, f32[192,2048]{1,0:T(8,128)}, u32[]{:S(2)}) %copy-start) | copy-done | bytes 1572888
  23.4 8.7 %shard_map.69 = (bf16[1,192,2,8,128]{4,3,2,1,0:T(8,128)(2,1)}, f32[192,192]{1,0:T(8,128)}) custom-call(f32[96,256]{1,0:T(8,128)S(1)} %get-tuple-element.4.packed_ref, f32[192,2048]{1,0:T(8,128)S(1)} %copy-done), custom_call_target="tpu_custom_call" | custom-call | tf_op jit(solution)/shard_map/pallas_call | solution.py:443
Async XLA Ops:
  22.0 1.4 %copy-start = (f32[192,2048]{1,0:T(8,128)S(1)}, f32[192,2048]{1,0:T(8,128)}, u32[]{:S(2)}) copy-start(f32[192,2048]{1,0:T(8,128)} %get-tuple-element.5.feature_in) | copy-start | bytes 4718596
